TPU v7x, 32 devices: a whole 2x2x4 slice. The times are simulated.
32 devices in a mesh: groups: 2 (over x), depth: 8 (over z, y), height: 2 (over core).
Axes of the slice: x: 2, y: 2, z: 4, core: 2. Of those that a mesh axis runs over, the one named last changes fastest.
Arguments:
- images: bfloat16 [4, 4, 64, 16, 256], P('groups', None, 'depth', 'height'), parts along dimension 0, may hold values from -6 to 6
- pre_hidden: bfloat16 [4, 16, 64, 16, 256], P('groups', None, 'depth', 'height'), parts along dimension 0, may hold values from -6 to 6
- pre_deep: bfloat16 [4, 32, 32, 8, 128], P(('groups', 'height'), None, 'depth'), parts along dimension 0, may hold values from -6 to 6
- pooled_grad: bfloat16 [4, 32, 16, 256], P(('groups', 'height'), None, 'depth'), parts along dimension 0, may hold values from -1.25 to 1.25
- deep_weight: bfloat16 [32, 16, 3, 3, 3], replicated, may hold values from -0.3125 to 0.3125
Outputs:
- first_kernel: float32 [32, 4, 3, 3, 3], P('groups'), parts along dimension 0
- first_bias: float32 [32], P('groups'), parts along dimension 0
- deep_kernel: float32 [64, 16, 3, 3, 3], P('groups'), parts along dimension 0
- deep_bias: float32 [64], P('groups'), parts along dimension 0
There are 2 independent parts, one for each index of `groups`. A program takes and returns all parts, laid end to end along the dimension named above; an argument that names none is the same for every part. Nothing has to cross between parts.
All inputs are finite; a program needn't handle non-finite values.
Results may differ from a plain program's by a relative error of at most 0.0031.
Values may be sent and summed in bfloat16 or wider, within the bound.
A program may use at most 128 MiB of HBM per device.

v0:
```python
import jax
import jax.numpy as jnp
from jax import lax
from jax.sharding import PartitionSpec as P

SLOPE = 0.3


def padded_2(block, sides, width):
    for axis, dim in sides:
        count = lax.axis_size(axis)
        forward = [(i, i + 1) for i in range(count - 1)]
        backward = [(target, source) for source, target in forward]
        low = lax.ppermute(
            lax.slice_in_dim(block, block.shape[dim] - width, None, axis=dim), axis, forward
        )
        high = lax.ppermute(lax.slice_in_dim(block, 0, width, axis=dim), axis, backward)
        block = jnp.concatenate([low, block, high], axis=dim)
    return block


def from_behind(value, axis, steps):
    count = lax.axis_size(axis)
    leading, last = (max(0, -steps), min(count, count - steps))
    return lax.ppermute(value, axis, [(source, source + steps) for source in range(leading, last)])


def leaky(values):
    return jnp.where(values > 0, values, SLOPE * values)


def slope_at(values):
    return jnp.where(values > 0, 1.0, SLOPE)


def deep_gradient(pooled_grad, pre_deep):
    samples, chans, quarter, flat = pooled_grad.shape
    half_depth, half_height, half_width = (pre_deep.shape[2], pre_deep.shape[3], pre_deep.shape[4])
    coarse = (
        pooled_grad.astype(jnp.float32).reshape(
            samples, chans, quarter, 1, half_height // 2, 1, half_width // 2, 1
        )
        / 8.0
    )
    spread = jnp.broadcast_to(
        coarse, (samples, chans, quarter, 2, half_height // 2, 2, half_width // 2, 2)
    )
    spread = spread.reshape(samples, chans, half_depth, half_height, half_width)
    return (spread * slope_at(pre_deep.astype(jnp.float32))).astype(jnp.bfloat16)


def deep_weight_grad(local_grad, padded):
    samples, chans = (padded.shape[0], padded.shape[1])
    coarse_depth, coarse_height, coarse_width = (
        local_grad.shape[2],
        local_grad.shape[3],
        local_grad.shape[4],
    )
    grown = jnp.pad(padded, ((0, 0), (0, 0), (0, 1), (0, 1), (0, 1)))
    phases = grown.reshape(
        samples, chans, coarse_depth + 1, 2, coarse_height + 1, 2, coarse_width + 1, 2
    )
    phases = phases.transpose(0, 1, 3, 5, 7, 2, 4, 6)
    kernels = []
    for depth_tap in range(3):
        for height_tap in range(3):
            for width_tap in range(3):
                depth_off, height_off, width_off = (depth_tap // 2, height_tap // 2, width_tap // 2)
                view = phases[
                    :,
                    :,
                    depth_tap % 2,
                    height_tap % 2,
                    width_tap % 2,
                    depth_off : depth_off + coarse_depth,
                    height_off : height_off + coarse_height,
                    width_off : width_off + coarse_width,
                ]
                kernels.append(
                    jnp.einsum(
                        "sodhw,sidhw->oi", local_grad, view, preferred_element_type=jnp.float32
                    )
                )
    kernel = jnp.stack(kernels, axis=-1).reshape(local_grad.shape[1], chans, 3, 3, 3)
    return (kernel, jnp.sum(local_grad, axis=(0, 2, 3, 4), dtype=jnp.float32))


def transpose_conv(extended, deep_weight):
    samples = extended.shape[0]
    coarse_depth, coarse_height, coarse_width = (
        extended.shape[2] - 1,
        extended.shape[3] - 1,
        extended.shape[4] - 1,
    )
    out_chans = deep_weight.shape[1]
    phase_taps = (((1, 0),), ((2, 0), (0, 1)))
    phases = []
    for depth_phase in range(2):
        for height_phase in range(2):
            for width_phase in range(2):
                views = []
                mats = []
                for depth_tap, depth_step in phase_taps[depth_phase]:
                    for height_tap, height_step in phase_taps[height_phase]:
                        for width_tap, width_step in phase_taps[width_phase]:
                            views.append(
                                extended[
                                    :,
                                    :,
                                    depth_step : depth_step + coarse_depth,
                                    height_step : height_step + coarse_height,
                                    width_step : width_step + coarse_width,
                                ]
                            )
                            mats.append(deep_weight[:, :, depth_tap, height_tap, width_tap])
                stacked = jnp.concatenate(views, axis=1)
                matrix = jnp.concatenate(mats, axis=0)
                phases.append(
                    jnp.einsum(
                        "sodhw,oi->sidhw", stacked, matrix, preferred_element_type=jnp.float32
                    )
                )
    grid = jnp.stack(phases, axis=0).reshape(
        2, 2, 2, samples, out_chans, coarse_depth, coarse_height, coarse_width
    )
    woven = grid.transpose(3, 4, 5, 0, 6, 1, 7, 2).reshape(
        samples, out_chans, 2 * coarse_depth, 2 * coarse_height, 2 * coarse_width
    )
    return woven.astype(jnp.bfloat16)


def first_weight_grad(first_grad, framed):
    chans = framed.shape[1]
    cells_depth, cells_height, cells_width = (
        first_grad.shape[2],
        first_grad.shape[3],
        first_grad.shape[4],
    )
    kernels = []
    for depth_tap in range(3):
        for height_tap in range(3):
            for width_tap in range(3):
                view = framed[
                    :,
                    :,
                    depth_tap : depth_tap + cells_depth,
                    height_tap : height_tap + cells_height,
                    width_tap : width_tap + cells_width,
                ]
                kernels.append(
                    jnp.einsum(
                        "sodhw,sidhw->oi", first_grad, view, preferred_element_type=jnp.float32
                    )
                )
    kernel = jnp.stack(kernels, axis=-1).reshape(first_grad.shape[1], chans, 3, 3, 3)
    return (kernel, jnp.sum(first_grad, axis=(0, 2, 3, 4), dtype=jnp.float32))


def on_device(images, pre_hidden, pre_deep, pooled_grad, deep_weight):
    deep_grad = deep_gradient(pooled_grad, pre_deep)
    hidden = leaky(pre_hidden.astype(jnp.float32)).astype(jnp.bfloat16)
    bordered = padded_2(images, (("depth", 2), ("height", 3)), 1)
    framed = jnp.pad(bordered, ((0, 0), (0, 0), (0, 0), (0, 0), (1, 1)))
    gathered = lax.all_to_all(hidden, "height", split_axis=0, concat_axis=3, tiled=True)
    below = from_behind(gathered[:, :, -1:], "depth", 1)
    padded = jnp.pad(
        jnp.concatenate([below, gathered], axis=2), ((0, 0), (0, 0), (0, 0), (1, 0), (1, 0))
    )
    above = from_behind(deep_grad[:, :, :1], "depth", -1)
    extended = jnp.pad(
        jnp.concatenate([deep_grad, above], axis=2), ((0, 0), (0, 0), (0, 0), (0, 1), (0, 1))
    )
    returned = transpose_conv(extended, deep_weight)
    hidden_grad = lax.all_to_all(returned, "height", split_axis=3, concat_axis=0, tiled=True)
    deep_kernel, deep_bias = deep_weight_grad(deep_grad, padded)
    first_grad = (
        hidden_grad.astype(jnp.float32) * slope_at(pre_hidden.astype(jnp.float32))
    ).astype(jnp.bfloat16)
    first_kernel, first_bias = first_weight_grad(first_grad, framed)
    first_kernel, first_bias, deep_kernel, deep_bias = lax.psum(
        (first_kernel, first_bias, deep_kernel, deep_bias), ("depth", "height")
    )
    return (first_kernel, first_bias, deep_kernel, deep_bias)


def solution(mesh):
    return jax.shard_map(
        on_device,
        mesh=mesh,
        in_specs=(
            P("groups", None, "depth", "height", None),
            P("groups", None, "depth", "height", None),
            P(("groups", "height"), None, "depth", None, None),
            P(("groups", "height"), None, "depth", None),
            P(),
        ),
        out_specs=(
            P("groups", None, None, None, None),
            P("groups"),
            P("groups", None, None, None, None),
            P("groups"),
        ),
        check_vma=False,
    )
```

profile of v0, /device:TPU:0, one launch (start us, length us, event | category | flops | bytes accessed | tf_op | source)
XLA Modules:
  0.0 230.6 jit_solution(8759666628445355263)
XLA Ops:
  0.6 1.2 copy.92
  2.5 1.3 collective-permute-start.2
  3.8 6.1 %collective-permute-start.1 = (bf16[2,4,1,8,256]{4,1,0,3,2:T(4,128)(2,1)}, bf16[2,4,1,8,256]{4,1,0,3,2:T(4,128)(2,1)}, u32[]{:S(2)}, u32[]{:S(2)}) collective-permute-start(bf16[2,4,1,8,256]{4,1,0,3,2:T(4,128)(2,1)} %get-tuple-element.24), channel_id=1, source_target_pairs={{0,2},{2,4},{4,6},{6,8},{8,10},{10,12},{12,14},{1,3},{3,5},{5,7},{... | collective-permute-start | bytes 98312 | tf_op jit(solution)/shard_map/ppermute | solution.py:14
  10.9 0.9 broadcast_in_dim.23
  13.2 1.3 collective-permute-start
  15.8 0.8 fusion.22
  16.7 0.8 concatenate.83
  18.3 1.2 constant_dynamic-update-slice_fusion.8
  21.0 2.1 collective-permute-start.3
  23.0 1.3 collective-permute-start.4
  28.2 14.3 %copy.88 = bf16[2,2,2,1,16,4,8,128]{4,2,7,1,6,0,5,3:T(2,128)(2,1)} copy(bf16[2,2,2,1,16,4,8,128]{7,4,6,5,2,1,0,3:T(8,128)(2,1)S(1)} %bitcast.783) | data formatting | bytes 2097152 | tf_op jit(solution)/shard_map/convert_element_type | solution.py:129
  42.5 6.9 %copy.89 = bf16[1,16,8,16,256]{4,2,1,0,3:T(8,128)(2,1)S(1)} copy(bf16[1,16,8,16,256]{1,4,3,2,0:T(8,128)(2,1)} %bitcast.752) | data formatting | bytes 2097152 | tf_op jit(solution)/shard_map/convert_element_type | solution.py:129
  49.4 5.9 %all_to_all.27 = bf16[1,16,8,16,256]{4,2,1,0,3:T(8,128)(2,1)S(1)} all-to-all(bf16[1,16,8,16,256]{4,2,1,0,3:T(8,128)(2,1)S(1)} %copy.89), channel_id=1, replica_groups=mesh['groups'=2,'depth'=8,'height'=2] {'height'}, dimensions={3} | all-to-all | bytes 2097152 | tf_op jit(solution)/shard_map/all_to_all | solution.py:174
  55.3 1.3 convert_reduce_fusion
  56.8 4.7 %all_to_all.28 = bf16[2,16,8,8,256]{4,3,2,1,0:T(8,128)(2,1)S(1)} all-to-all(bf16[2,16,8,8,256]{4,3,2,1,0:T(8,128)(2,1)S(1)} %copy.125), channel_id=1, replica_groups=mesh['groups'=2,'depth'=8,'height'=2] {'height'}, dimensions={0} | all-to-all | bytes 2097152 | tf_op jit(solution)/shard_map/all_to_all | solution.py:164
  61.6 4.9 %collective-permute-start.5 = (bf16[1,16,1,16,256]{4,3,2,1,0:T(8,128)(2,1)S(1)}, bf16[1,16,1,16,256]{4,3,2,1,0:T(8,128)(2,1)S(1)}, u32[]{:S(2)}, u32[]{:S(2)}) collective-permute-start(bf16[1,16,1,16,256]{4,3,2,1,0:T(8,128)(2,1)S(1)} %slice.448), channel_id=1, source_target_pairs={{0,2},{2,4},{4,6},{6,8},{8,10},{10,12},{12,14},{1,3},{3,5},{5,7},{... | collective-permute-start | bytes 393224 | tf_op jit(solution)/shard_map/ppermute | solution.py:25
  66.5 1.4 select_maximum_fusion
  68.7 1.6 fusion.81
  70.3 0.9 fusion.80
  71.1 0.8 fusion.79
  72.0 1.6 fusion.78
  73.6 0.9 fusion.77
  74.4 0.8 fusion.76
  75.2 1.6 fusion.75
  76.8 0.9 fusion.74
  77.7 0.8 fusion.73
  78.5 1.6 fusion.72
  80.1 0.9 fusion.71
  81.0 0.8 fusion.70
  81.8 0.9 fusion.69
  82.7 0.9 fusion.68
  83.5 0.8 fusion.67
  84.4 1.8 fusion.66
  86.2 0.9 fusion.65
  87.0 0.8 fusion.64
  87.9 1.6 fusion.63
  89.5 0.9 fusion.62
  90.3 0.8 fusion.61
  91.1 1.6 fusion.60
  92.7 0.9 fusion.59
  93.6 0.8 fusion.58
  94.4 1.6 fusion.57
  96.0 0.9 fusion.56
  97.0 6.6 %copy.193 = bf16[1,16,9,16,256]{1,4,3,2,0:T(8,128)(2,1)} copy(bf16[1,16,9,16,256]{4,3,2,1,0:T(8,128)(2,1)S(1)} %pad_maximum_fusion.4) | data formatting | bytes 2359296
  103.6 10.9 %pad.82 = bf16[1,16,10,18,258]{1,4,3,2,0:T(8,128)(2,1)} pad(bf16[1,16,9,16,256]{1,4,3,2,0:T(8,128)(2,1)} %copy.193, bf16[]{:T(256)} %constant.3.clone.1), padding=0_0x0_0x0_1x1_1x1_1 | pad | bytes 2665730 | tf_op jit(solution)/shard_map/jit(_pad)/pad | solution.py:59
  114.5 24.0 %reshape.237 = bf16[1,16,5,2,9,2,129,2]{1,7,6,5,4,3,2,0:T(2,128)(2,1)} reshape(bf16[1,16,10,18,258]{1,4,3,2,0:T(8,128)(2,1)} %pad.82) | data formatting | bytes 2972160 | tf_op jit(solution)/shard_map/reshape | solution.py:60
  138.5 22.6 %copy.128 = bf16[1,16,5,2,9,2,129,2]{6,1,4,2,7,5,3,0:T(8,128)(2,1)S(1)} copy(bf16[1,16,5,2,9,2,129,2]{1,7,6,5,4,3,2,0:T(2,128)(2,1)} %reshape.237) | data formatting | bytes 2972160 | tf_op jit(solution)/shard_map/reshape | solution.py:60
  166.9 63.7 %all-reduce.4 = (f32[16,4,3,3,3]{0,1,4,3,2:T(4,128)}, f32[16]{0:T(128)}, f32[32,16,3,3,3]{0,1,4,3,2:T(8,128)}, f32[32]{0:T(128)}) all-reduce(f32[16,4,3,3,3]{0,1,4,3,2:T(4,128)S(1)} %bitcast.786, f32[16]{0:T(128)S(1)} %get-tuple-element.10, ...), channel_id=1, replica_groups=mesh['groups'=2,'depth'=8,'height'=2] {'depth','height'}, use_global_device_ids=true, to_apply=%region_0.1 | all-reduce | flops 15600 | bytes 124800 | tf_op jit(solution)/shard_map/psum | solution.py:180
  (119 shorter events, 17.0 us)
Async XLA Ops:
  1.8 8.1 %copy-start.4 = (bf16[2,4,8,8,256]{4,1,0,3,2:T(4,128)(2,1)}, bf16[2,4,8,8,256]{4,1,0,3,2:T(4,128)(2,1)S(1)}, u32[]{:S(2)}) copy-start(bf16[2,4,8,8,256]{4,1,0,3,2:T(4,128)(2,1)S(1)} %copy.92) | copy-start | bytes 786436
  2.5 16.9 %collective-permute-start.2 = (bf16[2,4,1,8,256]{4,1,0,3,2:T(4,128)(2,1)}, bf16[2,4,1,8,256]{4,1,0,3,2:T(4,128)(2,1)}, u32[]{:S(2)}, u32[]{:S(2)}) collective-permute-start(bf16[2,4,1,8,256]{4,1,0,3,2:T(4,128)(2,1)} %get-tuple-element.23), channel_id=1, source_target_pairs={{2,0},{4,2},{6,4},{8,6},{10,8},{12,10},{14,12},{3,1},{5,3},{7,5},{... | collective-permute-start | bytes 98312 | tf_op jit(solution)/shard_map/ppermute | solution.py:17
  3.8 13.7 %collective-permute-start.1 = (bf16[2,4,1,8,256]{4,1,0,3,2:T(4,128)(2,1)}, bf16[2,4,1,8,256]{4,1,0,3,2:T(4,128)(2,1)}, u32[]{:S(2)}, u32[]{:S(2)}) collective-permute-start(bf16[2,4,1,8,256]{4,1,0,3,2:T(4,128)(2,1)} %get-tuple-element.24), channel_id=1, source_target_pairs={{0,2},{2,4},{4,6},{6,8},{8,10},{10,12},{12,14},{1,3},{3,5},{5,7},{... | collective-permute-start | bytes 98312 | tf_op jit(solution)/shard_map/ppermute | solution.py:14
  10.9 1.5 copy-start.6
  11.8 2.7 %copy-start.7 = (bf16[32,16,3,3,3]{0,1,4,3,2:T(8,128)(2,1)S(1)}, bf16[32,16,3,3,3]{0,1,4,3,2:T(8,128)(2,1)}, u32[]{:S(2)}) copy-start(bf16[32,16,3,3,3]{0,1,4,3,2:T(8,128)(2,1)} %param.9) | copy-start | bytes 82948
  13.2 11.2 %collective-permute-start = (bf16[1,32,1,8,128]{4,1,3,2,0:T(8,128)(2,1)S(1)}, bf16[1,32,1,8,128]{4,1,3,2,0:T(8,128)(2,1)S(1)}, u32[]{:S(2)}, u32[]{:S(2)}) collective-permute-start(bf16[1,32,1,8,128]{4,1,3,2,0:T(8,128)(2,1)S(1)} %slice.415), channel_id=1, source_target_pairs={{2,0},{4,2},{6,4},{8,6},{10,8},{12,10},{14,12},{3,1},{5,3},{7,5},{... | collective-permute-start | bytes 196616 | tf_op jit(solution)/shard_map/ppermute | solution.py:25
  20.2 4.9 %copy-start.2 = (bf16[2,4,10,8,256]{4,1,0,3,2:T(4,128)(2,1)}, bf16[2,4,10,8,256]{4,1,0,3,2:T(4,128)(2,1)S(1)}, u32[]{:S(2)}) copy-start(bf16[2,4,10,8,256]{4,1,0,3,2:T(4,128)(2,1)S(1)} %constant_dynamic-update-slice_fusion.7) | copy-start | bytes 983044
  21.0 45.5 %collective-permute-start.3 = (bf16[2,4,10,1,256]{4,1,0,3,2:T(4,128)(2,1)}, bf16[2,4,10,1,256]{4,1,0,3,2:T(4,128)(2,1)}, u32[]{:S(2)}, u32[]{:S(2)}) collective-permute-start(bf16[2,4,10,1,256]{4,1,0,3,2:T(4,128)(2,1)} %get-tuple-element.21), channel_id=1, source_target_pairs={{0,1},{2,3},{4,5},{6,7},{8,9},{10,11},{12,13},{14,15},{16,17},{18,... | collective-permute-start | bytes 122888 | tf_op jit(solution)/shard_map/ppermute | solution.py:14
  23.0 43.5 %collective-permute-start.4 = (bf16[2,4,10,1,256]{4,1,0,3,2:T(4,128)(2,1)}, bf16[2,4,10,1,256]{4,1,0,3,2:T(4,128)(2,1)}, u32[]{:S(2)}, u32[]{:S(2)}) collective-permute-start(bf16[2,4,10,1,256]{4,1,0,3,2:T(4,128)(2,1)} %get-tuple-element.22), channel_id=1, source_target_pairs={{1,0},{3,2},{5,4},{7,6},{9,8},{11,10},{13,12},{15,14},{17,16},{19,... | collective-permute-start | bytes 122888 | tf_op jit(solution)/shard_map/ppermute | solution.py:17
  24.8 0.9 copy-start.12
  24.8 0.9 copy-start.13
  24.9 1.1 copy-start.10
  24.9 1.1 copy-start.11
  25.1 1.2 copy-start.8
  25.2 1.2 copy-start.9
  25.2 1.2 copy-start.24
  25.2 1.2 copy-start.25
  26.0 0.7 copy-start.22
  26.1 0.7 copy-start.23
  26.4 0.7 copy-start.18
  26.4 0.7 copy-start.19
  26.4 0.7 copy-start.20
  26.4 0.7 copy-start.21
  26.8 0.7 copy-start.14
  26.8 0.7 copy-start.15
  26.8 0.7 copy-start.16
  26.8 0.7 copy-start.17
  49.4 5.9 %copy-start = (bf16[2,16,8,8,256]{4,3,2,1,0:T(8,128)(2,1)S(1)}, bf16[2,16,8,8,256]{4,3,2,1,0:T(8,128)(2,1)}, u32[]{:S(2)}) copy-start(bf16[2,16,8,8,256]{4,3,2,1,0:T(8,128)(2,1)} %param.6) | copy-start | bytes 3145732
  56.8 9.7 %copy-start.3 = (bf16[2,4,10,8,256]{4,1,0,3,2:T(4,128)(2,1)S(1)}, bf16[2,4,10,8,256]{4,1,0,3,2:T(4,128)(2,1)}, u32[]{:S(2)}) copy-start(bf16[2,4,10,8,256]{4,1,0,3,2:T(4,128)(2,1)} %copy-done.2) | copy-start | bytes 983044
  61.6 35.3 %collective-permute-start.5 = (bf16[1,16,1,16,256]{4,3,2,1,0:T(8,128)(2,1)S(1)}, bf16[1,16,1,16,256]{4,3,2,1,0:T(8,128)(2,1)S(1)}, u32[]{:S(2)}, u32[]{:S(2)}) collective-permute-start(bf16[1,16,1,16,256]{4,3,2,1,0:T(8,128)(2,1)S(1)} %slice.448), channel_id=1, source_target_pairs={{0,2},{2,4},{4,6},{6,8},{8,10},{10,12},{12,14},{1,3},{3,5},{5,7},{... | collective-permute-start | bytes 393224 | tf_op jit(solution)/shard_map/ppermute | solution.py:25
  70.3 1.7 copy-start.5
  80.1 1.7 copy-start.1
  164.7 2.2 copy-start.26
where the time goes:
time: 233 us; the launch traced here: 231 us
  local copies, waits for them, and re-layouts  95.9 us (41%)
  blocking collectives  74.3 us (32%)
  matrix products  37.7 us (16%)
  starting transfers between devices  16.9 us (7%)
  other arithmetic  4.49 us (2%)
    psum x1, blocking collectives, on_device(): lax.psum((first_kernel, first_bias, deep_kernel, deep_bias), ('depth', 'h...  63.7 us
    reshape x2, local copies, waits for them, and re-layouts, deep_weight_grad(): grown.reshape(samples, chans, coarse_depth + 1, 2, coarse_height + 1, 2,...  46.6 us
    dot_general x27, matrix products, first_weight_grad(): jnp.einsum('sodhw,sidhw->oi', first_grad, view, preferred_element_type=jn...  29 us
    convert_element_type x2, local copies, waits for them, and re-layouts, transpose_conv(): return woven.astype(jnp.bfloat16)  21.2 us
    pad x1, local copies, waits for them, and re-layouts, deep_weight_grad(): grown = jnp.pad(padded, ((0, 0), (0, 0), (0, 1), (0, 1), (0, 1)))  10.9 us
    unnamed x64, local copies, waits for them, and re-layouts  10.4 us
    ppermute x2, starting transfers between devices, padded_2(): lax.ppermute(lax.slice_in_dim(block, block.shape[dim] - width, None, axis...  8.18 us
    ppermute x2, starting transfers between devices, from_behind(): lax.ppermute(value, axis, [(source, source + steps) for source in range(l...  6.15 us
  transfers between devices with their start and end apart: 6, of which 0 were waited for; matrix products, arithmetic and copies ran while one was open for 29% of the time, Pallas kernels for 0%

commit v1 on v0

--- a/solution.py
+++ b/solution.py
@@ -171,7 +171,12 @@
         jnp.concatenate([deep_grad, above], axis=2), ((0, 0), (0, 0), (0, 0), (0, 1), (0, 1))
     )
     returned = transpose_conv(extended, deep_weight)
-    hidden_grad = lax.all_to_all(returned, "height", split_axis=3, concat_axis=0, tiled=True)
+    hidden_grad = jnp.concatenate(
+        lax.all_to_all(
+            jnp.stack(jnp.split(returned, lax.axis_size("height"), axis=3)), "height", 0, 0
+        ),
+        axis=0,
+    )
     deep_kernel, deep_bias = deep_weight_grad(deep_grad, padded)
     first_grad = (
         hidden_grad.astype(jnp.float32) * slope_at(pre_hidden.astype(jnp.float32))

time: 233 us -> 239 us (1.026)
  local copies, waits for them, and re-layouts: 95.9 us -> 102 us
    another operation x0 -> x3, local copies, waits for them, and re-layouts: none -> 13.3 us  [on_device(): jnp.stack(jnp.split(returned, lax.axis_size('height'), axis=3))]
    convert_element_type x2 -> x1, local copies, waits for them, and re-layouts: 21.2 us -> 14.3 us  [transpose_conv(): return woven.astype(jnp.bfloat16)]
  transfers between devices with their start and end apart: 6 -> 6, of which waited for: 0 -> 0; matrix products, arithmetic and copies ran while one was open for 29% -> 30% of each run, Pallas kernels for 0% -> 0%
where the time goes in v1:
time: 239 us; the launch traced here: 237 us
  local copies, waits for them, and re-layouts  102 us (43%)
  blocking collectives  74.3 us (31%)
  matrix products  37.7 us (16%)
  starting transfers between devices  16.9 us (7%)
  other arithmetic  4.23 us (2%)
    psum x1, blocking collectives, on_device(): lax.psum((first_kernel, first_bias, deep_kernel, deep_bias), ('depth', 'h...  63.7 us
    reshape x2, local copies, waits for them, and re-layouts, deep_weight_grad(): grown.reshape(samples, chans, coarse_depth + 1, 2, coarse_height + 1, 2,...  46.7 us
    dot_general x27, matrix products, first_weight_grad(): jnp.einsum('sodhw,sidhw->oi', first_grad, view, preferred_element_type=jn...  29 us
    convert_element_type x1, local copies, waits for them, and re-layouts, transpose_conv(): return woven.astype(jnp.bfloat16)  14.3 us
    another operation x3, local copies, waits for them, and re-layouts, on_device(): jnp.stack(jnp.split(returned, lax.axis_size('height'), axis=3))  13.3 us
    pad x1, local copies, waits for them, and re-layouts, deep_weight_grad(): grown = jnp.pad(padded, ((0, 0), (0, 0), (0, 1), (0, 1), (0, 1)))  11 us
    unnamed x64, local copies, waits for them, and re-layouts  10.5 us
    ppermute x2, starting transfers between devices, padded_2(): lax.ppermute(lax.slice_in_dim(block, block.shape[dim] - width, None, axis...  8.17 us
  transfers between devices with their start and end apart: 6, of which 0 were waited for; matrix products, arithmetic and copies ran while one was open for 30% of the time, Pallas kernels for 0%

profile of v1, /device:TPU:0, one launch (start us, length us, event | category | flops | bytes accessed | tf_op | source)
XLA Modules:
  0.0 236.7 jit_solution(16221054289293148030)
XLA Ops:
  0.6 1.2 copy.93
  2.5 1.3 collective-permute-start.2
  3.8 6.1 %collective-permute-start.1 = (bf16[2,4,1,8,256]{4,1,0,3,2:T(4,128)(2,1)}, bf16[2,4,1,8,256]{4,1,0,3,2:T(4,128)(2,1)}, u32[]{:S(2)}, u32[]{:S(2)}) collective-permute-start(bf16[2,4,1,8,256]{4,1,0,3,2:T(4,128)(2,1)} %get-tuple-element.26), channel_id=1, source_target_pairs={{0,2},{2,4},{4,6},{6,8},{8,10},{10,12},{12,14},{1,3},{3,5},{5,7},{... | collective-permute-start | bytes 98312 | tf_op jit(solution)/shard_map/ppermute | solution.py:14
  10.8 0.9 broadcast_in_dim.23
  13.2 1.3 collective-permute-start
  15.7 0.8 fusion.22
  18.2 1.2 constant_dynamic-update-slice_fusion.8
  20.9 2.1 collective-permute-start.3
  23.0 1.3 collective-permute-start.4
  28.1 14.3 %copy.90 = bf16[2,2,2,1,16,4,8,128]{4,2,7,1,6,0,5,3:T(2,128)(2,1)} copy(bf16[2,2,2,1,16,4,8,128]{7,4,6,5,2,1,0,3:T(8,128)(2,1)S(1)} %bitcast.782) | data formatting | bytes 2097152 | tf_op jit(solution)/shard_map/convert_element_type | solution.py:129
  42.4 6.0 %slice_bitcast_fusion.1 = (bf16[1,1,16,8,8,256]{2,5,4,3,1,0:T(8,128)(2,1)}, bf16[1,1,16,8,8,256]{2,5,4,3,1,0:T(8,128)(2,1)}) fusion(bf16[1,16,8,16,256]{1,4,3,2,0:T(8,128)(2,1)} %bitcast.751), kind=kLoop, calls=%fused_computation.1 | loop fusion | bytes 2097152 | tf_op jit(solution)/shard_map/stack | solution.py:176
  48.3 3.7 %copy.91 = bf16[1,1,16,8,8,256]{5,4,3,2,1,0:T(8,128)(2,1)S(1)} copy(bf16[1,1,16,8,8,256]{2,5,4,3,1,0:T(8,128)(2,1)} %get-tuple-element.14) | data formatting | bytes 1048576 | tf_op jit(solution)/shard_map/stack | solution.py:176
  52.0 3.7 %copy.92 = bf16[1,1,16,8,8,256]{5,4,3,2,1,0:T(8,128)(2,1)S(1)} copy(bf16[1,1,16,8,8,256]{2,5,4,3,1,0:T(8,128)(2,1)} %get-tuple-element.15) | data formatting | bytes 1048576 | tf_op jit(solution)/shard_map/stack | solution.py:176
  55.8 5.9 %all_to_all.23 = bf16[2,1,16,8,8,256]{5,4,3,2,1,0:T(8,128)(2,1)S(1)} all-to-all(bf16[2,1,16,8,8,256]{5,4,3,2,1,0:T(8,128)(2,1)S(1)} %pad_maximum_fusion.6), channel_id=1, replica_groups=mesh['groups'=2,'depth'=8,'height'=2] {'height'}, dimensions={0} | all-to-all | bytes 2097152 | tf_op jit(solution)/shard_map/all_to_all | solution.py:175
  61.8 1.0 convert_reduce_fusion
  62.7 4.7 %all_to_all.24 = bf16[2,16,8,8,256]{4,3,2,1,0:T(8,128)(2,1)S(1)} all-to-all(bf16[2,16,8,8,256]{4,3,2,1,0:T(8,128)(2,1)S(1)} %get-tuple-element.16), channel_id=1, replica_groups=mesh['groups'=2,'depth'=8,'height'=2] {'height'}, dimensions={0} | all-to-all | bytes 2097152 | tf_op jit(solution)/shard_map/all_to_all | solution.py:164
  67.5 4.9 %collective-permute-start.5 = (bf16[1,16,1,16,256]{4,3,2,1,0:T(8,128)(2,1)S(1)}, bf16[1,16,1,16,256]{4,3,2,1,0:T(8,128)(2,1)S(1)}, u32[]{:S(2)}, u32[]{:S(2)}) collective-permute-start(bf16[1,16,1,16,256]{4,3,2,1,0:T(8,128)(2,1)S(1)} %slice.448), channel_id=1, source_target_pairs={{0,2},{2,4},{4,6},{6,8},{8,10},{10,12},{12,14},{1,3},{3,5},{5,7},{... | collective-permute-start | bytes 393224 | tf_op jit(solution)/shard_map/ppermute | solution.py:25
  72.5 1.4 select_maximum_fusion
  74.6 1.6 fusion.81
  76.2 0.9 fusion.80
  77.1 0.8 fusion.79
  77.9 1.6 fusion.78
  79.5 0.9 fusion.77
  80.4 0.8 fusion.76
  81.2 1.6 fusion.75
  82.8 0.9 fusion.74
  83.6 0.8 fusion.73
  84.5 1.6 fusion.72
  86.1 0.9 fusion.71
  87.7 0.9 fusion.69
  88.6 0.9 fusion.68
  89.5 0.8 fusion.67
  90.3 1.8 fusion.66
  92.1 0.9 fusion.65
  93.0 0.8 fusion.64
  93.8 1.6 fusion.63
  95.4 0.9 fusion.62
  96.3 0.8 fusion.61
  97.1 1.6 fusion.60
  98.7 0.9 fusion.59
  99.5 0.8 fusion.58
  100.4 1.6 fusion.57
  102.0 0.9 fusion.56
  102.9 6.7 %copy.193 = bf16[1,16,9,16,256]{1,4,3,2,0:T(8,128)(2,1)} copy(bf16[1,16,9,16,256]{4,3,2,1,0:T(8,128)(2,1)S(1)} %pad_maximum_fusion.4) | data formatting | bytes 2359296
  109.6 11.0 %pad.84 = bf16[1,16,10,18,258]{1,4,3,2,0:T(8,128)(2,1)} pad(bf16[1,16,9,16,256]{1,4,3,2,0:T(8,128)(2,1)} %copy.193, bf16[]{:T(256)} %constant.3.clone.1), padding=0_0x0_0x0_1x1_1x1_1 | pad | bytes 2665730 | tf_op jit(solution)/shard_map/jit(_pad)/pad | solution.py:59
  120.6 24.0 %reshape.236 = bf16[1,16,5,2,9,2,129,2]{1,7,6,5,4,3,2,0:T(2,128)(2,1)} reshape(bf16[1,16,10,18,258]{1,4,3,2,0:T(8,128)(2,1)} %pad.84) | data formatting | bytes 2972160 | tf_op jit(solution)/shard_map/reshape | solution.py:60
  144.6 22.6 %copy.128 = bf16[1,16,5,2,9,2,129,2]{6,1,4,2,7,5,3,0:T(8,128)(2,1)S(1)} copy(bf16[1,16,5,2,9,2,129,2]{1,7,6,5,4,3,2,0:T(2,128)(2,1)} %reshape.236) | data formatting | bytes 2972160 | tf_op jit(solution)/shard_map/reshape | solution.py:60
  173.0 63.7 %all-reduce.4 = (f32[16,4,3,3,3]{0,1,4,3,2:T(4,128)}, f32[16]{0:T(128)}, f32[32,16,3,3,3]{0,1,4,3,2:T(8,128)}, f32[32]{0:T(128)}) all-reduce(f32[16,4,3,3,3]{0,1,4,3,2:T(4,128)S(1)} %bitcast.785, f32[16]{0:T(128)S(1)} %get-tuple-element.10, ...), channel_id=1, replica_groups=mesh['groups'=2,'depth'=8,'height'=2] {'depth','height'}, use_global_device_ids=true, to_apply=%region_0.1 | all-reduce | flops 15600 | bytes 124800 | tf_op jit(solution)/shard_map/psum | solution.py:185
  (121 shorter events, 18.6 us)
Async XLA Ops:
  1.8 8.1 %copy-start.4 = (bf16[2,4,8,8,256]{4,1,0,3,2:T(4,128)(2,1)}, bf16[2,4,8,8,256]{4,1,0,3,2:T(4,128)(2,1)S(1)}, u32[]{:S(2)}) copy-start(bf16[2,4,8,8,256]{4,1,0,3,2:T(4,128)(2,1)S(1)} %copy.93) | copy-start | bytes 786436
  2.5 16.9 %collective-permute-start.2 = (bf16[2,4,1,8,256]{4,1,0,3,2:T(4,128)(2,1)}, bf16[2,4,1,8,256]{4,1,0,3,2:T(4,128)(2,1)}, u32[]{:S(2)}, u32[]{:S(2)}) collective-permute-start(bf16[2,4,1,8,256]{4,1,0,3,2:T(4,128)(2,1)} %get-tuple-element.25), channel_id=1, source_target_pairs={{2,0},{4,2},{6,4},{8,6},{10,8},{12,10},{14,12},{3,1},{5,3},{7,5},{... | collective-permute-start | bytes 98312 | tf_op jit(solution)/shard_map/ppermute | solution.py:17
  3.8 13.6 %collective-permute-start.1 = (bf16[2,4,1,8,256]{4,1,0,3,2:T(4,128)(2,1)}, bf16[2,4,1,8,256]{4,1,0,3,2:T(4,128)(2,1)}, u32[]{:S(2)}, u32[]{:S(2)}) collective-permute-start(bf16[2,4,1,8,256]{4,1,0,3,2:T(4,128)(2,1)} %get-tuple-element.26), channel_id=1, source_target_pairs={{0,2},{2,4},{4,6},{6,8},{8,10},{10,12},{12,14},{1,3},{3,5},{5,7},{... | collective-permute-start | bytes 98312 | tf_op jit(solution)/shard_map/ppermute | solution.py:14
  10.8 1.5 copy-start.6
  11.8 2.7 %copy-start.7 = (bf16[32,16,3,3,3]{0,1,4,3,2:T(8,128)(2,1)S(1)}, bf16[32,16,3,3,3]{0,1,4,3,2:T(8,128)(2,1)}, u32[]{:S(2)}) copy-start(bf16[32,16,3,3,3]{0,1,4,3,2:T(8,128)(2,1)} %param.9) | copy-start | bytes 82948
  13.2 11.1 %collective-permute-start = (bf16[1,32,1,8,128]{4,1,3,2,0:T(8,128)(2,1)S(1)}, bf16[1,32,1,8,128]{4,1,3,2,0:T(8,128)(2,1)S(1)}, u32[]{:S(2)}, u32[]{:S(2)}) collective-permute-start(bf16[1,32,1,8,128]{4,1,3,2,0:T(8,128)(2,1)S(1)} %slice.415), channel_id=1, source_target_pairs={{2,0},{4,2},{6,4},{8,6},{10,8},{12,10},{14,12},{3,1},{5,3},{7,5},{... | collective-permute-start | bytes 196616 | tf_op jit(solution)/shard_map/ppermute | solution.py:25
  20.2 4.9 %copy-start.2 = (bf16[2,4,10,8,256]{4,1,0,3,2:T(4,128)(2,1)}, bf16[2,4,10,8,256]{4,1,0,3,2:T(4,128)(2,1)S(1)}, u32[]{:S(2)}) copy-start(bf16[2,4,10,8,256]{4,1,0,3,2:T(4,128)(2,1)S(1)} %constant_dynamic-update-slice_fusion.7) | copy-start | bytes 983044
  20.9 51.5 %collective-permute-start.3 = (bf16[2,4,10,1,256]{4,1,0,3,2:T(4,128)(2,1)}, bf16[2,4,10,1,256]{4,1,0,3,2:T(4,128)(2,1)}, u32[]{:S(2)}, u32[]{:S(2)}) collective-permute-start(bf16[2,4,10,1,256]{4,1,0,3,2:T(4,128)(2,1)} %get-tuple-element.23), channel_id=1, source_target_pairs={{0,1},{2,3},{4,5},{6,7},{8,9},{10,11},{12,13},{14,15},{16,17},{18,... | collective-permute-start | bytes 122888 | tf_op jit(solution)/shard_map/ppermute | solution.py:14
  23.0 49.5 %collective-permute-start.4 = (bf16[2,4,10,1,256]{4,1,0,3,2:T(4,128)(2,1)}, bf16[2,4,10,1,256]{4,1,0,3,2:T(4,128)(2,1)}, u32[]{:S(2)}, u32[]{:S(2)}) collective-permute-start(bf16[2,4,10,1,256]{4,1,0,3,2:T(4,128)(2,1)} %get-tuple-element.24), channel_id=1, source_target_pairs={{1,0},{3,2},{5,4},{7,6},{9,8},{11,10},{13,12},{15,14},{17,16},{19,... | collective-permute-start | bytes 122888 | tf_op jit(solution)/shard_map/ppermute | solution.py:17
  24.7 0.9 copy-start.12
  24.7 0.9 copy-start.13
  24.8 1.1 copy-start.10
  24.8 1.1 copy-start.11
  25.1 1.2 copy-start.8
  25.1 1.2 copy-start.9
  25.1 1.2 copy-start.24
  25.1 1.2 copy-start.25
  26.0 0.7 copy-start.22
  26.0 0.7 copy-start.23
  26.3 0.7 copy-start.18
  26.3 0.7 copy-start.19
  26.3 0.7 copy-start.20
  26.3 0.7 copy-start.21
  26.7 0.7 copy-start.14
  26.7 0.7 copy-start.15
  26.7 0.7 copy-start.16
  26.7 0.7 copy-start.17
  55.7 6.1 %copy-start = (bf16[2,16,8,8,256]{4,3,2,1,0:T(8,128)(2,1)S(1)}, bf16[2,16,8,8,256]{4,3,2,1,0:T(8,128)(2,1)}, u32[]{:S(2)}) copy-start(bf16[2,16,8,8,256]{4,3,2,1,0:T(8,128)(2,1)} %param.6) | copy-start | bytes 3145732
  62.7 9.7 %copy-start.3 = (bf16[2,4,10,8,256]{4,1,0,3,2:T(4,128)(2,1)S(1)}, bf16[2,4,10,8,256]{4,1,0,3,2:T(4,128)(2,1)}, u32[]{:S(2)}) copy-start(bf16[2,4,10,8,256]{4,1,0,3,2:T(4,128)(2,1)} %copy-done.2) | copy-start | bytes 983044
  67.5 35.3 %collective-permute-start.5 = (bf16[1,16,1,16,256]{4,3,2,1,0:T(8,128)(2,1)S(1)}, bf16[1,16,1,16,256]{4,3,2,1,0:T(8,128)(2,1)S(1)}, u32[]{:S(2)}, u32[]{:S(2)}) collective-permute-start(bf16[1,16,1,16,256]{4,3,2,1,0:T(8,128)(2,1)S(1)} %slice.448), channel_id=1, source_target_pairs={{0,2},{2,4},{4,6},{6,8},{8,10},{10,12},{12,14},{1,3},{3,5},{5,7},{... | collective-permute-start | bytes 393224 | tf_op jit(solution)/shard_map/ppermute | solution.py:25
  76.2 1.7 copy-start.5
  86.1 1.7 copy-start.1
  170.8 2.2 copy-start.26
